TPU v7x, 128 devices: a whole 4x4x4 slice. The times are simulated.
128 devices in a mesh: gy: 32 (over z, y, core), var: 4 (over x).
Axes of the slice: x: 4, y: 4, z: 4, core: 2. Of those that a mesh axis runs over, the one named last changes fastest.
Arguments:
- field: float32 [32, 32, 1024, 128], P('var', None, 'gy')
- factor_x: float32 [32, 16], replicated, may hold values from -1 to 1
- factor_y: float32 [1024, 64], P('gy'), may hold values from -0.1875 to 0.1875
- factor_z: float32 [128, 64], replicated, may hold values from -0.5 to 0.5
- factor_v: float32 [32, 16], replicated, may hold values from -1 to 1
Outputs:
- proj_z: float32 [128, 128], replicated
- proj_v: float32 [32, 32], replicated
- core_rms: float32 [], replicated
All inputs are finite; a program needn't handle non-finite values.
Results may differ from a plain program's by a relative error of at most 0.0003.
Values sent between devices are 32-bit elements; how exact they have to be, the bound alone decides.
No kernel may reach another device: no remote copies, remote signals or barrier semaphores. Data moves between devices by JAX's collectives and lax.ppermute only.
A program may use at most 192 MiB of HBM per device.

v0:
```python
import jax
import jax.numpy as jnp
from jax import lax
from jax.sharding import PartitionSpec as P

precise = lax.Precision.HIGHEST


def orth(mat):
    gram = jnp.dot(mat.T, mat, precision=precise)
    lower = jnp.linalg.cholesky(gram)
    return jax.scipy.linalg.solve_triangular(lower, mat.T, lower=True).T


def total_core(local_part):
    return lax.psum(local_part, ("gy", "var"))


def per_device(field, factor_x, factor_y, factor_z, factor_v):
    var_rows = field.shape[0]
    var_start = lax.axis_index("var") * var_rows
    local_v = lax.dynamic_slice_in_dim(factor_v, var_start, var_rows, 0)
    along_x = jnp.einsum("vxyz,xa->vayz", field, factor_x, precision=precise)
    partial_value = jnp.einsum("vayz,yb->vabz", along_x, factor_y, precision=precise)
    wide_z = jnp.einsum("vabz,vc->cabz", partial_value, local_v, precision=precise)
    fibres = lax.psum_scatter(wide_z, ("gy", "var"), scatter_dimension=3, tiled=True)
    z_count = fibres.shape[3]
    z_start = lax.axis_index(("gy", "var")) * z_count
    local_z = lax.dynamic_slice_in_dim(factor_z, z_start, z_count, 0)
    small_core = total_core(jnp.einsum("cabz,zr->cabr", fibres, local_z, precision=precise))
    rows_z = jnp.einsum("cabz,cabr->zr", fibres, small_core, precision=precise)
    raw_z = lax.all_gather(rows_z, ("gy", "var"), axis=0, tiled=True)
    new_z = orth(raw_z)
    proj_z = jnp.dot(new_z, new_z.T, precision=precise)
    wide_v = jnp.einsum("vabz,zr->vabr", partial_value, new_z, precision=precise)
    flat_v = wide_v.reshape(var_rows, -1)
    summed_v = lax.psum(flat_v, "gy")
    every_v = lax.all_gather(summed_v, "var", axis=0, tiled=True)
    gram_v = jnp.dot(every_v, every_v.T, precision=precise)
    new_v = orth(jnp.dot(gram_v, factor_v, precision=precise))
    proj_v = jnp.dot(new_v, new_v.T, precision=precise)
    core = jnp.dot(new_v.T, every_v, precision=precise)
    core_rms = jnp.sqrt(jnp.mean(core * core))
    return (proj_z, proj_v, core_rms)


def solution(mesh):
    in_specs = (P("var", None, "gy", None), P(), P("gy", None), P(), P())
    out_specs = (P(), P(), P())
    return jax.shard_map(
        per_device, mesh=mesh, in_specs=in_specs, out_specs=out_specs, check_vma=False
    )
```

profile of v0, /device:TPU:1, one launch (start us, length us, event | category | flops | bytes accessed | tf_op | source)
XLA Modules:
  0.0 1346.6 jit_solution(12369558590492828368)
XLA Ops:
  7.2 6.9 fusion.5
  14.1 4.1 convolution_bitcast_fusion
  18.2 2.0 copy-done.1
  20.2 5.2 copy.21
  25.4 122.6 %fusion.25 = f32[16,131072]{0,1} fusion(f32[8,131072]{1,0:T(8,128)} %bitcast.65, f32[32,16]{0,1:T(8,128)S(1)} %copy-done.3, s32[]{:T(128)S(6)} %select_n.14), kind=kOutput, calls=%fused_computation.35 | convolution fusion | flops 201326592 | bytes 71305216
  148.0 42.6 %copy.22 = f32[16,16,64,128]{2,1,0,3:T(8,128)} copy(f32[16,16,64,128]{0,3,2,1:T(8,128)} %bitcast.7) | data formatting | bytes 16777216 | tf_op jit(solution)/shard_map/vabz,vc->cabz/dot_general | solution.py:25
  190.9 668.2 %reduce-scatter.2.cloned.1.call-done = f32[16,16,64,1]{2,1,0,3:T(8,128)} async-done(((f32[16,16,64,128]{2,1,0,3:T(8,128)}), f32[16,16,64,1]{2,1,0,3:T(8,128)}) %reduce-scatter.2.cloned.1.call-update) | async-done | bytes 65552 | tf_op jit(solution)/shard_map/reduce_scatter | solution.py:26
  859.1 5.5 broadcast_multiply_fusion
  864.7 165.4 %all-reduce.4.cloned.1.call-done = f32[16,16,64,64]{3,2,1,0:T(8,128)} async-done(((f32[16,16,64,64]{3,2,1,0:T(8,128)}), f32[16,16,64,64]{3,2,1,0:T(8,128)}) %all-reduce.4.cloned.1.call-update) | async-done | bytes 4194320 | tf_op jit(solution)/shard_map/psum | solution.py:16
  1030.1 6.6 fusion.9
  1037.0 64.0 %all-reduce = f32[8192]{0:T(1024)S(1)} all-reduce(f32[8192]{0:T(1024)S(1)} %dynamic-update-slice.6), channel_id=2, replica_groups=mesh['gy'=32,'var'=4] {'gy','var'}, use_global_device_ids=true, to_apply=%add | all-reduce | flops 8192 | bytes 65536
  1101.5 5.8 cholesky.29
  1108.0 0.7 fusion.13
  1108.7 4.9 custom-call.14
  1113.9 6.6 fusion.14
  1120.5 4.7 reshape.38
  1125.3 104.6 %all-reduce.6.cloned.1.call-done = f32[8,65536]{1,0:T(8,128)} async-done(((f32[8,65536]{1,0:T(8,128)}), f32[8,65536]{1,0:T(8,128)}) %all-reduce.6.cloned.1.call-update) | async-done | bytes 2097168 | tf_op jit(solution)/shard_map/psum | solution.py:37
  1229.9 0.9 fusion.29
  1230.8 83.4 %all-gather.3.cloned.1.call-done = f32[32,65536]{1,0:T(8,128)} async-done(((f32[8,65536]{1,0:T(8,128)}), f32[32,65536]{1,0:T(8,128)}) %all-gather.3.cloned.1.call-update) | async-done | bytes 8388624 | tf_op jit(solution)/shard_map/all_gather | solution.py:38
  1314.2 10.7 fusion.30
  1325.2 1.5 cholesky.61
  1328.0 1.2 custom-call.15
  1329.5 0.8 fusion.33
  1330.3 7.5 fusion.8
  (35 shorter events, 4.0 us)
Async XLA Ops:
  7.2 183.6 %copy-start = (f32[128,64]{0,1:T(8,128)S(1)}, f32[128,64]{0,1:T(8,128)}, u32[]{:S(2)}) copy-start(f32[128,64]{0,1:T(8,128)} %param.8) | copy-start | bytes 98308
  7.2 6.9 copy-start.4
  7.2 851.9 %reduce-scatter.2.cloned.1.call-start = ((), (), s32[]{:S(2)}) async-start(), calls=%async_computation.1 | async-start | bytes 16908288 | tf_op jit(solution)/shard_map/reduce_scatter | solution.py:26
  18.2 2.0 copy-start.1
  20.2 5.3 copy-start.3
  190.7 839.4 %all-reduce.4.cloned.1.call-start = ((), (), s32[]{:S(2)}) async-start(), calls=%async_computation.2 | async-start | bytes 16777216 | tf_op jit(solution)/shard_map/psum | solution.py:16
  864.6 165.5 %copy-start.2 = (f32[16,16,64,1]{2,1,0,3:T(8,128)S(1)}, f32[16,16,64,1]{2,1,0,3:T(8,128)}, u32[]{:S(2)}) copy-start(f32[16,16,64,1]{2,1,0,3:T(8,128)} %reduce-scatter.2.cloned.1.call-done) | copy-start | bytes 196612
  864.6 365.3 %all-reduce.6.cloned.1.call-start = ((), (), s32[]{:S(2)}) async-start(), calls=%async_computation.3 | async-start | bytes 4194304 | tf_op jit(solution)/shard_map/psum | solution.py:37
  1125.2 189.0 %all-gather.3.cloned.1.call-start = ((), (), s32[]{:S(2)}) async-start(), calls=%async_computation.4 | async-start | bytes 10485760 | tf_op jit(solution)/shard_map/all_gather | solution.py:38
Sparse Core Ops, SparseCore 0:
  190.8 668.2 reduce-scatter.1
  864.7 165.3 all-reduce.3
  1125.3 104.5 all-reduce.5
  1231.5 82.6 all-gather.2
where the time goes:
time: 1350 us
  waiting for transfers between devices  1020 us (76%)
  matrix products  168 us (12%)
  blocking collectives  64 us (5%)
  local copies, waits for them, and re-layouts  55.3 us (4%)
  other arithmetic  21.6 us (2%)
  between operations  16.2 us (1%)
    reduce_scatter x1, waiting for transfers between devices, per_device(): lax.psum_scatter(wide_z, ('gy', 'var'), scatter_dimension=3, tiled=True)  668 us
    psum x1, waiting for transfers between devices, total_core(): return lax.psum(local_part, ('gy', 'var'))  165 us
    unnamed x1, matrix products  123 us
    psum x1, waiting for transfers between devices, per_device(): summed_v = lax.psum(flat_v, 'gy')  105 us
    all_gather x1, waiting for transfers between devices, per_device(): every_v = lax.all_gather(summed_v, 'var', axis=0, tiled=True)  83.4 us
    unnamed x1, blocking collectives  64 us
    dot_general x1, local copies, waits for them, and re-layouts, per_device(): jnp.einsum('vabz,vc->cabz', partial_value, local_v, precision=precise)  42.6 us
  transfers between devices with their start and end apart: 4, of which 4 were waited for; matrix products, arithmetic and copies ran while one was open for 0% of the time, Pallas kernels for 0%

commit v1 on v0

--- a/solution.py
+++ b/solution.py
@@ -35,7 +35,12 @@
     wide_v = jnp.einsum("vabz,zr->vabr", partial_value, new_z, precision=precise)
     flat_v = wide_v.reshape(var_rows, -1)
     summed_v = lax.psum(flat_v, "gy")
-    every_v = lax.all_gather(summed_v, "var", axis=0, tiled=True)
+    ring = [summed_v]
+    for hop in range(3):
+        ring.append(lax.ppermute(ring[-1], "var", [(dev, (dev + 1) % 4) for dev in range(4)]))
+    every_v = jnp.roll(
+        jnp.concatenate(ring[::-1], axis=0), (lax.axis_index("var") + 1) * ring[0].shape[0], axis=0
+    )
     gram_v = jnp.dot(every_v, every_v.T, precision=precise)
     new_v = orth(jnp.dot(gram_v, factor_v, precision=precise))
     proj_v = jnp.dot(new_v, new_v.T, precision=precise)

time: 1350 us -> 1410 us (1.044)
  waiting for transfers between devices: 1020 us -> 1080 us
  matrix products: 168 us -> 153 us
  local copies, waits for them, and re-layouts: 55.3 us -> 69.8 us
    ppermute x0 -> x3, waiting for transfers between devices: none -> 139 us  [per_device(): lax.ppermute(ring[-1], 'var', [(dev, (dev + 1) % 4) for dev in range(4)])]
    all_gather x1 -> x0, waiting for transfers between devices: 83.4 us -> none  [per_device(): every_v = lax.all_gather(summed_v, 'var', axis=0, tiled=True)]
    unnamed x12 -> x25, local copies, waits for them, and re-layouts: 2.26 us -> 16.6 us
  transfers between devices with their start and end apart: 4 -> 6, of which waited for: 4 -> 6; matrix products, arithmetic and copies ran while one was open for 0% -> 0% of each run, Pallas kernels for 0% -> 0%
where the time goes in v1:
time: 1410 us; the launch traced here: 1400 us
  waiting for transfers between devices  1080 us (77%)
  matrix products  153 us (11%)
  local copies, waits for them, and re-layouts  69.8 us (5%)
  blocking collectives  64.1 us (5%)
  other arithmetic  21.7 us (2%)
  between operations  16 us (1%)
    reduce_scatter x1, waiting for transfers between devices, per_device(): lax.psum_scatter(wide_z, ('gy', 'var'), scatter_dimension=3, tiled=True)  667 us
    psum x1, waiting for transfers between devices, total_core(): return lax.psum(local_part, ('gy', 'var'))  166 us
    ppermute x3, waiting for transfers between devices, per_device(): lax.ppermute(ring[-1], 'var', [(dev, (dev + 1) % 4) for dev in range(4)])  139 us
    unnamed x1, matrix products  111 us
    psum x1, waiting for transfers between devices, per_device(): summed_v = lax.psum(flat_v, 'gy')  105 us
    unnamed x1, blocking collectives  64.1 us
    dot_general x1, local copies, waits for them, and re-layouts, per_device(): jnp.einsum('vabz,vc->cabz', partial_value, local_v, precision=precise)  42.7 us
  transfers between devices with their start and end apart: 6, of which 6 were waited for; matrix products, arithmetic and copies ran while one was open for 0% of the time, Pallas kernels for 0%

profile of v1, /device:TPU:1, one launch (start us, length us, event | category | flops | bytes accessed | tf_op | source)
XLA Modules:
  0.0 1403.0 jit_solution(3712999605808720583)
XLA Ops:
  7.2 6.9 fusion.8
  14.1 4.8 convolution_bitcast_fusion
  18.9 2.0 copy-done.1
  20.9 5.2 copy.21
  26.2 111.2 %fusion.30 = f32[16,131072]{0,1} fusion(f32[8,131072]{1,0:T(8,128)} %bitcast.62, f32[32,16]{0,1:T(8,128)S(1)} %copy-done.7, s32[]{:T(128)S(6)} %select_n.27), kind=kOutput, calls=%fused_computation.46 | convolution fusion | flops 201326592 | bytes 71305216
  137.3 42.7 %copy.22 = f32[16,16,64,128]{2,1,0,3:T(8,128)} copy(f32[16,16,64,128]{0,3,2,1:T(8,128)} %bitcast.7) | data formatting | bytes 16777216 | tf_op jit(solution)/shard_map/vabz,vc->cabz/dot_general | solution.py:25
  180.3 667.3 %reduce-scatter.2.cloned.1.call-done = f32[16,16,64,1]{2,1,0,3:T(8,128)} async-done(((f32[16,16,64,128]{2,1,0,3:T(8,128)}), f32[16,16,64,1]{2,1,0,3:T(8,128)}) %reduce-scatter.2.cloned.1.call-update) | async-done | bytes 65552 | tf_op jit(solution)/shard_map/reduce_scatter | solution.py:26
  847.5 5.5 broadcast_multiply_fusion
  853.2 166.2 %all-reduce.4.cloned.1.call-done = f32[16,16,64,64]{3,2,1,0:T(8,128)} async-done(((f32[16,16,64,64]{3,2,1,0:T(8,128)}), f32[16,16,64,64]{3,2,1,0:T(8,128)}) %all-reduce.4.cloned.1.call-update) | async-done | bytes 4194320 | tf_op jit(solution)/shard_map/psum | solution.py:16
  1019.3 6.6 fusion.14
  1026.2 64.1 %all-reduce = f32[8192]{0:T(1024)S(1)} all-reduce(f32[8192]{0:T(1024)S(1)} %dynamic-update-slice.6), channel_id=2, replica_groups=mesh['gy'=32,'var'=4] {'gy','var'}, use_global_device_ids=true, to_apply=%add | all-reduce | flops 8192 | bytes 65536
  1090.7 5.8 cholesky.29
  1097.9 4.9 custom-call.14
  1103.1 6.6 fusion.19
  1109.7 4.7 reshape.38
  1114.4 104.7 %all-reduce.6.cloned.1.call-done = f32[8,65536]{1,0:T(8,128)} async-done(((f32[8,65536]{1,0:T(8,128)}), f32[8,65536]{1,0:T(8,128)}) %all-reduce.6.cloned.1.call-update) | async-done | bytes 2097168 | tf_op jit(solution)/shard_map/psum | solution.py:37
  1220.3 46.7 %collective-permute-done = f32[8,65536]{1,0:T(8,128)S(1)} collective-permute-done((f32[8,65536]{1,0:T(8,128)}, f32[8,65536]{1,0:T(8,128)S(1)}, u32[]{:S(2)}, u32[]{:S(2)}) %collective-permute-start) | collective-permute-done | bytes 2097184 | tf_op jit(solution)/shard_map/ppermute | solution.py:40
  1268.4 46.9 %collective-permute-done.1 = f32[8,65536]{1,0:T(8,128)} collective-permute-done((f32[8,65536]{1,0:T(8,128)S(1)}, f32[8,65536]{1,0:T(8,128)}, u32[]{:S(2)}, u32[]{:S(2)}) %collective-permute-start.1) | collective-permute-done | bytes 2097184 | tf_op jit(solution)/shard_map/ppermute | solution.py:40
  1316.4 45.2 %collective-permute-done.2 = f32[8,65536]{1,0:T(8,128)} collective-permute-done((f32[8,65536]{1,0:T(8,128)}, f32[8,65536]{1,0:T(8,128)}, u32[]{:S(2)}, u32[]{:S(2)}) %collective-permute-start.2) | collective-permute-done | bytes 2097184 | tf_op jit(solution)/shard_map/ppermute | solution.py:40
  1363.3 1.7 constant_dynamic-update-slice_fusion.6
  1365.4 1.7 constant_dynamic-update-slice_fusion.3
  1369.2 5.7 copy-done.2
  1374.9 6.6 fusion.3
  1386.1 7.5 fusion.11
  (52 shorter events, 15.7 us)
Async XLA Ops:
  7.2 172.9 %copy-start = (f32[128,64]{0,1:T(8,128)S(1)}, f32[128,64]{0,1:T(8,128)}, u32[]{:S(2)}) copy-start(f32[128,64]{0,1:T(8,128)} %param.8) | copy-start | bytes 98308
  7.2 840.4 %reduce-scatter.2.cloned.1.call-start = ((), (), s32[]{:S(2)}) async-start(), calls=%async_computation.1 | async-start | bytes 16908288 | tf_op jit(solution)/shard_map/reduce_scatter | solution.py:26
  14.1 12.1 copy-start.7
  18.9 2.0 copy-start.1
  180.0 839.3 %all-reduce.4.cloned.1.call-start = ((), (), s32[]{:S(2)}) async-start(), calls=%async_computation.2 | async-start | bytes 16777216 | tf_op jit(solution)/shard_map/psum | solution.py:16
  847.5 171.8 %copy-start.6 = (f32[16,16,64,1]{2,1,0,3:T(8,128)S(1)}, f32[16,16,64,1]{2,1,0,3:T(8,128)}, u32[]{:S(2)}) copy-start(f32[16,16,64,1]{2,1,0,3:T(8,128)} %reduce-scatter.2.cloned.1.call-done) | copy-start | bytes 196612
  853.1 366.0 %all-reduce.6.cloned.1.call-start = ((), (), s32[]{:S(2)}) async-start(), calls=%async_computation.3 | async-start | bytes 4194304 | tf_op jit(solution)/shard_map/psum | solution.py:37
  1219.1 146.1 %copy-start.3 = (f32[8,65536]{1,0:T(8,128)S(1)}, f32[8,65536]{1,0:T(8,128)}, u32[]{:S(2)}) copy-start(f32[8,65536]{1,0:T(8,128)} %all-reduce.6.cloned.1.call-done) | copy-start | bytes 6291460
  1219.1 47.9 %collective-permute-start = (f32[8,65536]{1,0:T(8,128)}, f32[8,65536]{1,0:T(8,128)S(1)}, u32[]{:S(2)}, u32[]{:S(2)}) collective-permute-start(f32[8,65536]{1,0:T(8,128)} %all-reduce.6.cloned.1.call-done), channel_id=1, source_target_pairs={{0,1},{1,2},{2,3},{3,0},{4,5},{5,6},{6,7},{7,4},{8,9},{9,10},{10,1... | collective-permute-start | bytes 6291464 | tf_op jit(solution)/shard_map/ppermute | solution.py:40
  1267.0 1.3 copy-start.4
  1268.4 46.9 %collective-permute-start.1 = (f32[8,65536]{1,0:T(8,128)S(1)}, f32[8,65536]{1,0:T(8,128)}, u32[]{:S(2)}, u32[]{:S(2)}) collective-permute-start(f32[8,65536]{1,0:T(8,128)S(1)} %collective-permute-done), channel_id=1, source_target_pairs={{0,1},{1,2},{2,3},{3,0},{4,5},{5,6},{6,7},{7,4},{8,9},{9,10},{10,1... | collective-permute-start | bytes 6291464 | tf_op jit(solution)/shard_map/ppermute | solution.py:40
  1315.3 46.3 %collective-permute-start.2 = (f32[8,65536]{1,0:T(8,128)}, f32[8,65536]{1,0:T(8,128)}, u32[]{:S(2)}, u32[]{:S(2)}) collective-permute-start(f32[8,65536]{1,0:T(8,128)} %collective-permute-done.1), channel_id=1, source_target_pairs={{0,1},{1,2},{2,3},{3,0},{4,5},{5,6},{6,7},{7,4},{8,9},{9,10},{10,1... | collective-permute-start | bytes 6291464 | tf_op jit(solution)/shard_map/ppermute | solution.py:40
  1315.5 49.6 %copy-start.5 = (f32[8,65536]{1,0:T(8,128)S(1)}, f32[8,65536]{1,0:T(8,128)}, u32[]{:S(2)}) copy-start(f32[8,65536]{1,0:T(8,128)} %copy-done.4) | copy-start | bytes 6291460
  1369.1 5.7 copy-start.2
Sparse Core Ops, SparseCore 0:
  180.1 667.3 reduce-scatter.1
  853.2 166.0 all-reduce.3
  1114.5 104.5 all-reduce.5

commit v2 on v0

--- a/solution.py
+++ b/solution.py
@@ -34,7 +34,9 @@
     proj_z = jnp.dot(new_z, new_z.T, precision=precise)
     wide_v = jnp.einsum("vabz,zr->vabr", partial_value, new_z, precision=precise)
     flat_v = wide_v.reshape(var_rows, -1)
-    summed_v = lax.psum(flat_v, "gy")
+    summed_v = flat_v
+    for hop in (1, 2, 4, 8, 16):
+        summed_v = summed_v + lax.ppermute(summed_v, "gy", [(dev, dev ^ hop) for dev in range(32)])
     every_v = lax.all_gather(summed_v, "var", axis=0, tiled=True)
     gram_v = jnp.dot(every_v, every_v.T, precision=precise)
     new_v = orth(jnp.dot(gram_v, factor_v, precision=precise))

time: 1350 us -> 1430 us (1.059)
  waiting for transfers between devices: 1020 us -> 1100 us
    ppermute x0 -> x5, waiting for transfers between devices: none -> 183 us  [per_device(): lax.ppermute(summed_v, 'gy', [(dev, dev ^ hop) for dev in range(32)])]
    psum x1 -> x0, waiting for transfers between devices: 105 us -> none  [per_device(): summed_v = lax.psum(flat_v, 'gy')]
  transfers between devices with their start and end apart: 4 -> 8, of which waited for: 4 -> 8; matrix products, arithmetic and copies ran while one was open for 0% -> 0% of each run, Pallas kernels for 0% -> 0%
where the time goes in v2:
time: 1430 us; the launch traced here: 1420 us
  waiting for transfers between devices  1100 us (77%)
  matrix products  156 us (11%)
  blocking collectives  64.1 us (4%)
  local copies, waits for them, and re-layouts  54 us (4%)
  other arithmetic  24.1 us (2%)
  between operations  15.9 us (1%)
    reduce_scatter x1, waiting for transfers between devices, per_device(): lax.psum_scatter(wide_z, ('gy', 'var'), scatter_dimension=3, tiled=True)  667 us
    ppermute x5, waiting for transfers between devices, per_device(): lax.ppermute(summed_v, 'gy', [(dev, dev ^ hop) for dev in range(32)])  183 us
    psum x1, waiting for transfers between devices, total_core(): return lax.psum(local_part, ('gy', 'var'))  166 us
    unnamed x1, matrix products  111 us
    all_gather x1, waiting for transfers between devices, per_device(): every_v = lax.all_gather(summed_v, 'var', axis=0, tiled=True)  83.1 us
    unnamed x1, blocking collectives  64.1 us
    dot_general x1, local copies, waits for them, and re-layouts, per_device(): jnp.einsum('vabz,vc->cabz', partial_value, local_v, precision=precise)  42.7 us
  transfers between devices with their start and end apart: 8, of which 8 were waited for; matrix products, arithmetic and copies ran while one was open for 0% of the time, Pallas kernels for 0%

profile of v2, /device:TPU:1, one launch (start us, length us, event | category | flops | bytes accessed | tf_op | source)
XLA Modules:
  0.0 1419.7 jit_solution(8883208184153728233)
XLA Ops:
  7.2 6.9 fusion.5
  14.1 4.1 convolution_bitcast_fusion
  18.2 2.0 copy-done.1
  20.2 5.2 copy.21
  25.5 111.2 %fusion.25 = f32[16,131072]{0,1} fusion(f32[8,131072]{1,0:T(8,128)} %bitcast.65, f32[32,16]{0,1:T(8,128)S(1)} %copy-done.3, s32[]{:T(128)S(6)} %select_n.14), kind=kOutput, calls=%fused_computation.35 | convolution fusion | flops 201326592 | bytes 71305216
  136.6 42.7 %copy.22 = f32[16,16,64,128]{2,1,0,3:T(8,128)} copy(f32[16,16,64,128]{0,3,2,1:T(8,128)} %bitcast.7) | data formatting | bytes 16777216 | tf_op jit(solution)/shard_map/vabz,vc->cabz/dot_general | solution.py:25
  179.5 666.6 %reduce-scatter.2.cloned.1.call-done = f32[16,16,64,1]{2,1,0,3:T(8,128)} async-done(((f32[16,16,64,128]{2,1,0,3:T(8,128)}), f32[16,16,64,1]{2,1,0,3:T(8,128)}) %reduce-scatter.2.cloned.1.call-update) | async-done | bytes 65552 | tf_op jit(solution)/shard_map/reduce_scatter | solution.py:26
  846.2 5.5 broadcast_multiply_fusion
  851.7 165.8 %all-reduce.3.cloned.1.call-done = f32[16,16,64,64]{3,2,1,0:T(8,128)} async-done(((f32[16,16,64,64]{3,2,1,0:T(8,128)}), f32[16,16,64,64]{3,2,1,0:T(8,128)}) %all-reduce.3.cloned.1.call-update) | async-done | bytes 4194320 | tf_op jit(solution)/shard_map/psum | solution.py:16
  1017.6 6.6 fusion.9
  1024.5 64.1 %all-reduce = f32[8192]{0:T(1024)S(1)} all-reduce(f32[8192]{0:T(1024)S(1)} %dynamic-update-slice.6), channel_id=2, replica_groups=mesh['gy'=32,'var'=4] {'gy','var'}, use_global_device_ids=true, to_apply=%add | all-reduce | flops 8192 | bytes 65536
  1089.0 5.8 cholesky.29
  1096.2 4.9 custom-call.14
  1101.4 6.6 fusion.14
  1107.9 3.4 reshape.38
  1112.1 3.8 collective-permute-done
  1117.1 46.0 %collective-permute-done.1 = f32[8,65536]{1,0:T(8,128)S(1)} collective-permute-done((f32[8,65536]{1,0:T(8,128)S(1)}, f32[8,65536]{1,0:T(8,128)S(1)}, u32[]{:S(2)}, u32[]{:S(2)}) %collective-permute-start.1) | collective-permute-done | bytes 2097184 | tf_op jit(solution)/shard_map/ppermute | solution.py:39
  1165.1 45.6 %collective-permute-done.2 = f32[8,65536]{1,0:T(8,128)S(1)} collective-permute-done((f32[8,65536]{1,0:T(8,128)S(1)}, f32[8,65536]{1,0:T(8,128)S(1)}, u32[]{:S(2)}, u32[]{:S(2)}) %collective-permute-start.2) | collective-permute-done | bytes 2097184 | tf_op jit(solution)/shard_map/ppermute | solution.py:39
  1212.1 44.2 %collective-permute-done.3 = f32[8,65536]{1,0:T(8,128)S(1)} collective-permute-done((f32[8,65536]{1,0:T(8,128)S(1)}, f32[8,65536]{1,0:T(8,128)S(1)}, u32[]{:S(2)}, u32[]{:S(2)}) %collective-permute-start.3) | collective-permute-done | bytes 2097184 | tf_op jit(solution)/shard_map/ppermute | solution.py:39
  1256.5 2.0 collective-permute-start.4
  1258.5 43.7 %collective-permute-done.4 = f32[8,65536]{1,0:T(8,128)S(1)} collective-permute-done((f32[8,65536]{1,0:T(8,128)S(1)}, f32[8,65536]{1,0:T(8,128)S(1)}, u32[]{:S(2)}, u32[]{:S(2)}) %collective-permute-start.4) | collective-permute-done | bytes 2097184 | tf_op jit(solution)/shard_map/ppermute | solution.py:39
  1304.7 83.1 %all-gather.3.cloned.1.call-done = f32[32,65536]{1,0:T(8,128)} async-done(((f32[8,65536]{1,0:T(8,128)}), f32[32,65536]{1,0:T(8,128)}) %all-gather.3.cloned.1.call-update) | async-done | bytes 8388624 | tf_op jit(solution)/shard_map/all_gather | solution.py:40
  1387.8 10.4 fusion.30
  1403.6 7.5 fusion.8
  (47 shorter events, 16.1 us)
Async XLA Ops:
  7.2 172.2 %copy-start = (f32[128,64]{0,1:T(8,128)S(1)}, f32[128,64]{0,1:T(8,128)}, u32[]{:S(2)}) copy-start(f32[128,64]{0,1:T(8,128)} %param.8) | copy-start | bytes 98308
  7.2 6.9 copy-start.4
  7.2 839.0 %reduce-scatter.2.cloned.1.call-start = ((), (), s32[]{:S(2)}) async-start(), calls=%async_computation.1 | async-start | bytes 16908288 | tf_op jit(solution)/shard_map/reduce_scatter | solution.py:26
  18.2 2.0 copy-start.1
  20.2 5.3 copy-start.3
  179.3 838.3 %all-reduce.3.cloned.1.call-start = ((), (), s32[]{:S(2)}) async-start(), calls=%async_computation.2 | async-start | bytes 16777216 | tf_op jit(solution)/shard_map/psum | solution.py:16
  851.7 165.9 %copy-start.2 = (f32[16,16,64,1]{2,1,0,3:T(8,128)S(1)}, f32[16,16,64,1]{2,1,0,3:T(8,128)}, u32[]{:S(2)}) copy-start(f32[16,16,64,1]{2,1,0,3:T(8,128)} %reduce-scatter.2.cloned.1.call-done) | copy-start | bytes 196612
  851.7 536.1 %all-gather.3.cloned.1.call-start = ((), (), s32[]{:S(2)}) async-start(), calls=%async_computation.3 | async-start | bytes 10485760 | tf_op jit(solution)/shard_map/all_gather | solution.py:40
  1111.3 4.5 collective-permute-start
  1116.1 46.9 %collective-permute-start.1 = (f32[8,65536]{1,0:T(8,128)S(1)}, f32[8,65536]{1,0:T(8,128)S(1)}, u32[]{:S(2)}, u32[]{:S(2)}) collective-permute-start(f32[8,65536]{1,0:T(8,128)S(1)} %add.56), channel_id=1, source_target_pairs={{0,8},{4,12},{8,0},{12,4},{16,24},{20,28},{24,16},{28,20},{32,40},... | collective-permute-start | bytes 6291464 | tf_op jit(solution)/shard_map/ppermute | solution.py:39
  1163.3 47.5 %collective-permute-start.2 = (f32[8,65536]{1,0:T(8,128)S(1)}, f32[8,65536]{1,0:T(8,128)S(1)}, u32[]{:S(2)}, u32[]{:S(2)}) collective-permute-start(f32[8,65536]{1,0:T(8,128)S(1)} %add.57), channel_id=1, source_target_pairs={{0,16},{4,20},{8,24},{12,28},{16,0},{20,4},{24,8},{28,12},{32,48},... | collective-permute-start | bytes 6291464 | tf_op jit(solution)/shard_map/ppermute | solution.py:39
  1211.0 45.3 %collective-permute-start.3 = (f32[8,65536]{1,0:T(8,128)S(1)}, f32[8,65536]{1,0:T(8,128)S(1)}, u32[]{:S(2)}, u32[]{:S(2)}) collective-permute-start(f32[8,65536]{1,0:T(8,128)S(1)} %add.58), channel_id=1, source_target_pairs={{0,32},{4,36},{8,40},{12,44},{16,48},{20,52},{24,56},{28,60},{32,0... | collective-permute-start | bytes 6291464 | tf_op jit(solution)/shard_map/ppermute | solution.py:39
  1256.5 45.7 %collective-permute-start.4 = (f32[8,65536]{1,0:T(8,128)S(1)}, f32[8,65536]{1,0:T(8,128)S(1)}, u32[]{:S(2)}, u32[]{:S(2)}) collective-permute-start(f32[8,65536]{1,0:T(8,128)S(1)} %add.59), channel_id=1, source_target_pairs={{0,64},{4,68},{8,72},{12,76},{16,80},{20,84},{24,88},{28,92},{32,9... | collective-permute-start | bytes 6291464 | tf_op jit(solution)/shard_map/ppermute | solution.py:39
Sparse Core Ops, SparseCore 0:
  179.4 666.7 reduce-scatter.1
  851.8 165.7 all-reduce.2
  1303.9 83.8 all-gather.2
